TPU v7x, 512 devices: a whole 4x4x16 slice. The times are simulated.
512 devices in a mesh: kp: 32 (over z, x_hi), kz: 16 (over y, x_lo, core).
Axes of the slice: x: 4 (x_hi: 2, x_lo: 2; x = x_hi * 2 + x_lo), y: 4, z: 16, core: 2. Of those that a mesh axis runs over, the one named last changes fastest.
Arguments:
- orbitals: bfloat16 [32, 16, 2, 64, 1024], P('kp', 'kz'), may hold values from -0.75 to 0.75
- trial_vectors: bfloat16 [32, 16, 2, 2, 1024], P('kp', 'kz'), may hold values from -6 to 6
- screened_table: bfloat16 [256, 2, 1024, 1024], P('kp', None, 'kz'), may hold values from -0.09375 to 0.09375
- shift_inplane: int32 [2], replicated, may hold values from -128 to 127
- shift_depth: int32 [2], replicated, may hold values from -64 to 63
- table_entry: int32 [2], replicated, may hold values from 0 to 255
Outputs:
- kernel_image: float32 [32, 16, 2, 2, 1024], P('kp', 'kz')
All inputs are finite; a program needn't handle non-finite values.
Results may differ from a plain program's by a relative error of at most 0.0049.
Values may be sent and summed in bfloat16 or wider, within the bound.
A program may use at most 64 MiB of HBM per device.

v0:
```python
import jax
import jax.numpy as jnp
from jax import lax
from jax.sharding import PartitionSpec as P

NV = 32


def spread(shard, axis, root):
    mine = lax.axis_index(axis) == root
    return lax.psum(jnp.where(mine, shard, jnp.zeros_like(shard)), axis)


def passed_along(block, axis, distance):
    devices = range(lax.axis_size(axis))
    route = [((i - distance) % len(devices), i) for i in devices]
    return lax.ppermute(block, axis, route)


def pair_term(own_valence, own_conduction, next_valence, next_conduction, next_trial, screen_rows):
    valence_count = own_valence.shape[1]
    conduction_count = own_conduction.shape[1]
    row_span = own_conduction.shape[2]
    points = own_valence.shape[2]
    vector_count = next_trial.shape[0]
    trial_matrix = next_trial.reshape(vector_count, 2, conduction_count, valence_count)
    real_part = jnp.swapaxes(trial_matrix[:, 0], 1, 2)
    imag_part = jnp.swapaxes(trial_matrix[:, 1], 1, 2)
    upper_rows = jnp.concatenate([real_part, -imag_part], axis=2)
    lower_rows = jnp.concatenate([imag_part, real_part], axis=2)
    coeffs = jnp.stack([upper_rows, lower_rows], axis=1).reshape(
        vector_count * 2 * valence_count, 2 * conduction_count
    )
    amplitude = jnp.dot(
        coeffs,
        next_conduction.reshape(2 * conduction_count, row_span),
        preferred_element_type=jnp.float32,
    )
    amplitude = amplitude.astype(jnp.bfloat16).reshape(vector_count, 2, valence_count, row_span)
    partner_rows = next_valence.reshape(2 * valence_count, points)
    own_real = own_valence[0]
    own_imag = own_valence[1]
    valence_stack = jnp.concatenate(
        [
            jnp.concatenate([own_real, -own_imag], axis=1),
            jnp.concatenate([own_imag, own_real], axis=1),
        ],
        axis=0,
    )
    block = min(512, row_span)

    def one_vector(amplitude_pair):
        amp_real = amplitude_pair[0]
        amp_imag = amplitude_pair[1]

        def add_block(block_index, accumulated):
            row_start = block_index * block
            part_real = lax.dynamic_slice_in_dim(amp_real, row_start, block, 1)
            part_imag = lax.dynamic_slice_in_dim(amp_imag, row_start, block, 1)
            left_factor = jnp.concatenate(
                [
                    jnp.concatenate([part_real, part_imag], axis=0),
                    jnp.concatenate([part_imag, -part_real], axis=0),
                ],
                axis=1,
            )
            expanded = lax.dot_general(
                left_factor,
                partner_rows,
                (((0,), (0,)), ((), ())),
                preferred_element_type=jnp.float32,
            )
            exp_real = expanded[:block]
            exp_imag = expanded[block:]
            screen_part = lax.dynamic_slice_in_dim(screen_rows, row_start, block, 1)
            w_real = screen_part[0].astype(jnp.float32)
            w_imag = screen_part[1].astype(jnp.float32)
            product = jnp.concatenate(
                [w_real * exp_real - w_imag * exp_imag, w_real * exp_imag + w_imag * exp_real],
                axis=1,
            ).astype(jnp.bfloat16)
            half_product = lax.dot_general(
                product, valence_stack, (((1,), (1,)), ((), ())), preferred_element_type=jnp.float32
            ).astype(jnp.bfloat16)
            half_real = half_product[:, :valence_count]
            half_imag = half_product[:, valence_count:]
            half_stack = jnp.concatenate(
                [
                    jnp.concatenate([half_real, half_imag], axis=1),
                    jnp.concatenate([half_imag, -half_real], axis=1),
                ],
                axis=0,
            )
            cond_part = lax.dynamic_slice_in_dim(own_conduction, row_start, block, 2)
            cond_cat = jnp.concatenate([cond_part[0], cond_part[1]], axis=1)
            return accumulated + jnp.dot(cond_cat, half_stack, preferred_element_type=jnp.float32)

        result = lax.fori_loop(
            0,
            row_span // block,
            add_block,
            jnp.zeros((conduction_count, 2 * valence_count), jnp.float32),
        )
        return jnp.stack(
            [result[:, :valence_count].reshape(-1), result[:, valence_count:].reshape(-1)]
        )

    return lax.map(one_vector, amplitude)


def shards(orbitals, trial_vectors, screened_table, shift_inplane, shift_depth, table_entry):
    slot_count = screened_table.shape[0]
    valence_count = NV
    plane_size = lax.axis_size("kp")
    depth_size = lax.axis_size("kz")
    plane_offsets = shift_inplane % plane_size
    depth_offsets = shift_depth % depth_size
    rows_list = []
    carried_list = []
    for transfer in range(2):
        target = table_entry[transfer]
        stored_slab = lax.dynamic_index_in_dim(
            screened_table, target % slot_count, 0, keepdims=False
        )
        rows_list.append(spread(stored_slab, "kp", target // slot_count))
        carried = (orbitals, trial_vectors)
        for bit_level in range((plane_size - 1).bit_length()):
            arrived = passed_along((carried[0], carried[1]), "kp", -(1 << bit_level))
            chosen = plane_offsets[transfer] // (1 << bit_level) % 2 == 1
            carried = (
                jnp.where(chosen, arrived[0], carried[0]),
                jnp.where(chosen, arrived[1], carried[1]),
            )
        carried_list.append(carried)
    own_orbitals = orbitals[0, 0]
    accumulated = jnp.zeros(trial_vectors.shape[2:], jnp.float32)
    for transfer in range(2):
        carried = carried_list[transfer]
        for bit_level in range((depth_size - 1).bit_length()):
            arrived = passed_along((carried[0], carried[1]), "kz", -(1 << bit_level))
            chosen = depth_offsets[transfer] // (1 << bit_level) % 2 == 1
            carried = (
                jnp.where(chosen, arrived[0], carried[0]),
                jnp.where(chosen, arrived[1], carried[1]),
            )
        full_screen = lax.all_gather(rows_list[transfer], "kz", axis=1, tiled=True)
        partner = carried[0][0, 0]
        accumulated = accumulated + pair_term(
            own_orbitals[:, :valence_count],
            own_orbitals[:, valence_count:],
            partner[:, :valence_count],
            partner[:, valence_count:],
            carried[1][0, 0],
            full_screen,
        )
    return accumulated[None, None]


def solution(mesh):
    in_specs = (
        P("kp", "kz", None, None, None),
        P("kp", "kz", None, None, None),
        P("kp", None, "kz", None),
        P(),
        P(),
        P(),
    )
    out_specs = P("kp", "kz", None, None, None)
    return jax.shard_map(shards, mesh=mesh, in_specs=in_specs, out_specs=out_specs, check_vma=False)
```

profile of v0, /device:TPU:70, one launch (start us, length us, event | category | flops | bytes accessed | tf_op | source)
XLA Modules:
  0.0 690.1 jit_solution(12332485336313917325)
XLA Ops:
  36.6 11.4 %collective-permute-start.1 = (bf16[1,1,2,2,1024]{4,3,2,1,0:T(2,128)(2,1)S(1)}, bf16[1,1,2,2,1024]{4,3,2,1,0:T(2,128)(2,1)S(1)}, u32[]{:S(2)}, u32[]{:S(2)}) collective-permute-start(bf16[1,1,2,2,1024]{4,3,2,1,0:T(2,128)(2,1)S(1)} %get-tuple-element.532), channel_id=1, source_target_pairs={{32,0},{48,16},{64,32},{80,48},{96,64},{112,80},{128,96},{144,112}... | collective-permute-start | bytes 24584 | tf_op jit(solution)/shard_map/ppermute | solution.py:17
  51.5 4.6 collective-permute-start.2
  56.0 278.9 %all-reduce.3.cloned.1.call-done = (bf16[2,64,1024]{2,0,1:T(2,128)(2,1)}, bf16[2,64,1024]{2,0,1:T(2,128)(2,1)}) async-done(((bf16[2,64,1024]{2,0,1:T(2,128)(2,1)}, bf16[2,64,1024]{2,0,1:T(2,128)(2,1)}), (bf16[2,64,1024]{2,0,1:T(2,128)(2,1)}, bf16[2,64,1024]{2,0,1:T(2,128)(2,1)})) %all-reduce.3.cloned.1.call-update) | async-done | bytes 524304 | tf_op jit(solution)/shard_map/psum | solution.py:11
  335.0 4.8 collective-permute-start.20
  339.8 6.5 collective-permute-start.3
  346.3 6.9 %collective-permute-start.21 = (bf16[1,1,2,2,1024]{4,3,2,1,0:T(2,128)(2,1)S(1)}, bf16[1,1,2,2,1024]{4,3,2,1,0:T(2,128)(2,1)S(1)}, u32[]{:S(2)}, u32[]{:S(2)}) collective-permute-start(bf16[1,1,2,2,1024]{4,3,2,1,0:T(2,128)(2,1)S(1)} %broadcast_select_fusion.21), channel_id=1, source_target_pairs={{256,0},{272,16},{288,32},{304,48},{320,64},{336,80},{352,96},{368... | collective-permute-start | bytes 24584 | tf_op jit(solution)/shard_map/ppermute | solution.py:17
  353.3 7.6 %collective-permute-start.4 = (bf16[1,1,2,2,1024]{4,3,2,1,0:T(2,128)(2,1)S(1)}, bf16[1,1,2,2,1024]{4,3,2,1,0:T(2,128)(2,1)S(1)}, u32[]{:S(2)}, u32[]{:S(2)}) collective-permute-start(bf16[1,1,2,2,1024]{4,3,2,1,0:T(2,128)(2,1)S(1)} %broadcast_select_fusion.30), channel_id=1, source_target_pairs={{256,0},{272,16},{288,32},{304,48},{320,64},{336,80},{352,96},{368... | collective-permute-start | bytes 24584 | tf_op jit(solution)/shard_map/ppermute | solution.py:17
  362.9 4.6 collective-permute-done.4
  372.3 5.3 collective-permute-start.6
  387.6 4.5 collective-permute-start.8
  398.2 5.1 collective-permute-done.26
  410.6 5.9 collective-permute-start.11
  416.5 10.2 %collective-permute-done.27 = bf16[1,1,2,64,1024]{4,3,2,1,0:T(8,128)(2,1)S(1)} collective-permute-done((bf16[1,1,2,64,1024]{4,3,2,1,0:T(8,128)(2,1)S(1)}, bf16[1,1,2,64,1024]{4,3,2,1,0:T(8,128)(2,1)S(1)}, u32[]{:S(2)}, u32[]{:S(2)}) %collective-permute-start.27) | collective-permute-done | bytes 262176 | tf_op jit(solution)/shard_map/ppermute | solution.py:17
  426.8 5.0 collective-permute-start.28
  431.9 28.6 %collective-permute-done.11 = bf16[1,1,2,64,1024]{4,3,2,1,0:T(8,128)(2,1)S(1)} collective-permute-done((bf16[1,1,2,64,1024]{4,3,2,1,0:T(8,128)(2,1)S(1)}, bf16[1,1,2,64,1024]{4,3,2,1,0:T(8,128)(2,1)S(1)}, u32[]{:S(2)}, u32[]{:S(2)}) %collective-permute-start.11) | collective-permute-done | bytes 262176 | tf_op jit(solution)/shard_map/ppermute | solution.py:17
  462.5 5.4 collective-permute-start.29
  468.0 50.9 %collective-permute-done.12 = bf16[1,1,2,64,1024]{4,3,2,1,0:T(8,128)(2,1)S(1)} collective-permute-done((bf16[1,1,2,64,1024]{4,3,2,1,0:T(8,128)(2,1)S(1)}, bf16[1,1,2,64,1024]{4,3,2,1,0:T(8,128)(2,1)S(1)}, u32[]{:S(2)}, u32[]{:S(2)}) %collective-permute-start.12) | collective-permute-done | bytes 262176 | tf_op jit(solution)/shard_map/ppermute | solution.py:17
  518.9 8.7 %collective-permute-start.13 = (bf16[1,1,2,64,1024]{4,3,2,1,0:T(8,128)(2,1)S(1)}, bf16[1,1,2,64,1024]{4,3,2,1,0:T(8,128)(2,1)S(1)}, u32[]{:S(2)}, u32[]{:S(2)}) collective-permute-start(bf16[1,1,2,64,1024]{4,3,2,1,0:T(8,128)(2,1)S(1)} %broadcast_select_fusion.13), channel_id=1, source_target_pairs={{256,0},{272,16},{288,32},{304,48},{320,64},{336,80},{352,96},{368... | collective-permute-start | bytes 786440 | tf_op jit(solution)/shard_map/ppermute | solution.py:17
  529.7 6.3 collective-permute-done.13
  542.9 14.9 %collective-permute-start.15 = (bf16[1,1,2,64,1024]{4,3,2,1,0:T(8,128)(2,1)S(1)}, bf16[1,1,2,64,1024]{4,3,2,1,0:T(8,128)(2,1)S(1)}, u32[]{:S(2)}, u32[]{:S(2)}) collective-permute-start(bf16[1,1,2,64,1024]{4,3,2,1,0:T(8,128)(2,1)S(1)} %broadcast_select_fusion.15), channel_id=1, source_target_pairs={{2,0},{3,1},{4,2},{5,3},{6,4},{7,5},{8,6},{9,7},{10,8},{11,9},{12,... | collective-permute-start | bytes 786440 | tf_op jit(solution)/shard_map/ppermute | solution.py:17
  557.8 9.6 %collective-permute-start.32 = (bf16[1,1,2,64,1024]{4,3,2,1,0:T(8,128)(2,1)S(1)}, bf16[1,1,2,64,1024]{4,3,2,1,0:T(8,128)(2,1)S(1)}, u32[]{:S(2)}, u32[]{:S(2)}) collective-permute-start(bf16[1,1,2,64,1024]{4,3,2,1,0:T(8,128)(2,1)S(1)} %broadcast_select_fusion.8), channel_id=1, source_target_pairs={{4,0},{5,1},{6,2},{7,3},{8,4},{9,5},{10,6},{11,7},{12,8},{13,9},{1... | collective-permute-start | bytes 786440 | tf_op jit(solution)/shard_map/ppermute | solution.py:17
  567.6 5.0 collective-permute-start.16
  576.5 10.1 %collective-permute-done.16 = bf16[1,1,2,64,1024]{4,3,2,1,0:T(8,128)(2,1)S(1)} collective-permute-done((bf16[1,1,2,64,1024]{4,3,2,1,0:T(8,128)(2,1)S(1)}, bf16[1,1,2,64,1024]{4,3,2,1,0:T(8,128)(2,1)S(1)}, u32[]{:S(2)}, u32[]{:S(2)}) %collective-permute-start.16) | collective-permute-done | bytes 262176 | tf_op jit(solution)/shard_map/ppermute | solution.py:17
  588.7 13.3 %collective-permute-done.17 = bf16[1,1,2,64,1024]{4,3,2,1,0:T(8,128)(2,1)S(1)} collective-permute-done((bf16[1,1,2,64,1024]{4,3,2,1,0:T(8,128)(2,1)S(1)}, bf16[1,1,2,64,1024]{4,3,2,1,0:T(8,128)(2,1)S(1)}, u32[]{:S(2)}, u32[]{:S(2)}) %collective-permute-start.17) | collective-permute-done | bytes 262176 | tf_op jit(solution)/shard_map/ppermute | solution.py:17
  602.5 11.3 %copy.28 = bf16[2,1024,1024]{1,2,0:T(8,128)(2,1)} copy(bf16[2,1024,1024]{2,0,1:T(2,128)(2,1)} %all-gather.5.cloned.1.call-done) | data formatting | bytes 8388608 | tf_op jit(solution)/shard_map/while | solution.py:108
  613.7 29.2 %while.51 = (s32[]{:T(128)}, f32[2,2,1024]{2,1,0:T(2,128)S(1)}, bf16[2,2,32,1024]{3,2,1,0:T(8,128)(2,1)S(1)}, bf16[2,32,1024]{2,1,0:T(8,128)(2,1)S(1)}, bf16[2,1...) while((s32[]{:T(128)}, f32[2,2,1024]{2,1,0:T(2,128)S(1)}, ...), condition=%wide.region_9.10_spmd, body=%wide.region_6.9_spmd.sunk | while | flops 283219968 | bytes 16187882 | solution.py:108
  613.8 14.3 %while.53 = (s32[]{:T(128)}, f32[32,64]{1,0:T(8,128)S(1)}, bf16[2,32,1024]{2,1,0:T(8,128)(2,1)S(1)}, bf16[2,1024,1024]{1,2,0:T(8,128)(2,1)}, bf16[32,1024]{1,0:T...) while((s32[]{:T(128)}, f32[32,64]{1,0:T(8,128)S(1)}, ...), condition=%wide.region_8.8_spmd.clone, body=%wide.region_7.7_spmd.clone.sunk | while | flops 283217920 | bytes 15876309 | solution.py:98
  628.4 14.3 %while.53 = (s32[]{:T(128)}, f32[32,64]{1,0:T(8,128)S(1)}, bf16[2,32,1024]{2,1,0:T(8,128)(2,1)S(1)}, bf16[2,1024,1024]{1,2,0:T(8,128)(2,1)}, bf16[32,1024]{1,0:T...) while((s32[]{:T(128)}, f32[32,64]{1,0:T(8,128)S(1)}, ...), condition=%wide.region_8.8_spmd.clone, body=%wide.region_7.7_spmd.clone.sunk | while | flops 283217920 | bytes 15876309 | solution.py:98
  643.0 11.2 %copy.23 = bf16[2,1024,1024]{1,2,0:T(8,128)(2,1)} copy(bf16[2,1024,1024]{2,0,1:T(2,128)(2,1)} %all-gather.3.cloned.1.call-done) | data formatting | bytes 8388608 | tf_op jit(solution)/shard_map/while | solution.py:108
  654.2 28.8 %while.49 = (s32[]{:T(128)}, f32[2,2,1024]{2,1,0:T(2,128)S(1)}, bf16[2,2,32,1024]{3,2,1,0:T(8,128)(2,1)S(1)}, bf16[2,32,1024]{2,1,0:T(8,128)(2,1)S(1)}, bf16[2,1...) while((s32[]{:T(128)}, f32[2,2,1024]{2,1,0:T(2,128)S(1)}, ...), condition=%wide.region_4.5_spmd, body=%wide.region_1.4_spmd.sunk | while | flops 283219968 | bytes 16187882 | solution.py:108
  654.2 14.1 %while.52 = (s32[]{:T(128)}, f32[32,64]{1,0:T(8,128)S(1)}, bf16[2,32,1024]{2,1,0:T(8,128)(2,1)S(1)}, bf16[2,1024,1024]{1,2,0:T(8,128)(2,1)}, bf16[32,1024]{1,0:T...) while((s32[]{:T(128)}, f32[32,64]{1,0:T(8,128)S(1)}, ...), condition=%wide.region_3.3_spmd.clone, body=%wide.region_2.2_spmd.clone.sunk | while | flops 283217920 | bytes 15876309 | solution.py:98
  668.6 14.1 %while.52 = (s32[]{:T(128)}, f32[32,64]{1,0:T(8,128)S(1)}, bf16[2,32,1024]{2,1,0:T(8,128)(2,1)S(1)}, bf16[2,1024,1024]{1,2,0:T(8,128)(2,1)}, bf16[32,1024]{1,0:T...) while((s32[]{:T(128)}, f32[32,64]{1,0:T(8,128)S(1)}, ...), condition=%wide.region_3.3_spmd.clone, body=%wide.region_2.2_spmd.clone.sunk | while | flops 283217920 | bytes 15876309 | solution.py:98
  (206 shorter events, 123.2 us)
Async XLA Ops:
  6.5 328.3 %all-reduce.3.cloned.1.call-start = ((), (), s32[]{:S(2)}) async-start(), calls=%async_computation.2 | async-start | bytes 1048576 | tf_op jit(solution)/shard_map/psum | solution.py:11
  6.5 385.6 %collective-permute-start.9 = (bf16[1,1,2,64,1024]{4,3,2,1,0:T(8,128)(2,1)}, bf16[1,1,2,64,1024]{4,3,2,1,0:T(8,128)(2,1)S(1)}, u32[]{:S(2)}, u32[]{:S(2)}) collective-permute-start(bf16[1,1,2,64,1024]{4,3,2,1,0:T(8,128)(2,1)} %param.14), channel_id=1, source_target_pairs={{16,0},{32,16},{48,32},{64,48},{80,64},{96,80},{112,96},{128,112},... | collective-permute-start | bytes 786440 | tf_op jit(solution)/shard_map/ppermute | solution.py:17
  10.0 22.0 %collective-permute-start = (bf16[1,1,2,2,1024]{4,3,2,1,0:T(2,128)(2,1)}, bf16[1,1,2,2,1024]{4,3,2,1,0:T(2,128)(2,1)S(1)}, u32[]{:S(2)}, u32[]{:S(2)}) collective-permute-start(bf16[1,1,2,2,1024]{4,3,2,1,0:T(2,128)(2,1)} %param.15), channel_id=1, source_target_pairs={{16,0},{32,16},{48,32},{64,48},{80,64},{96,80},{112,96},{128,112},... | collective-permute-start | bytes 24584 | tf_op jit(solution)/shard_map/ppermute | solution.py:17
  22.4 580.1 %all-gather.5.cloned.1.call-start = ((), (), s32[]{:S(2)}) async-start(), calls=%async_computation.1 | async-start | bytes 4456448 | tf_op jit(solution)/shard_map/all_gather | solution.py:146
  32.0 16.0 %collective-permute-start.18 = (bf16[1,1,2,2,1024]{4,3,2,1,0:T(2,128)(2,1)S(1)}, bf16[1,1,2,2,1024]{4,3,2,1,0:T(2,128)(2,1)S(1)}, u32[]{:S(2)}, u32[]{:S(2)}) collective-permute-start(bf16[1,1,2,2,1024]{4,3,2,1,0:T(2,128)(2,1)S(1)} %get-tuple-element.531), channel_id=1, source_target_pairs={{32,0},{48,16},{64,32},{80,48},{96,64},{112,80},{128,96},{144,112}... | collective-permute-start | bytes 24584 | tf_op jit(solution)/shard_map/ppermute | solution.py:17
  36.6 14.8 %collective-permute-start.1 = (bf16[1,1,2,2,1024]{4,3,2,1,0:T(2,128)(2,1)S(1)}, bf16[1,1,2,2,1024]{4,3,2,1,0:T(2,128)(2,1)S(1)}, u32[]{:S(2)}, u32[]{:S(2)}) collective-permute-start(bf16[1,1,2,2,1024]{4,3,2,1,0:T(2,128)(2,1)S(1)} %get-tuple-element.532), channel_id=1, source_target_pairs={{32,0},{48,16},{64,32},{80,48},{96,64},{112,80},{128,96},{144,112}... | collective-permute-start | bytes 24584 | tf_op jit(solution)/shard_map/ppermute | solution.py:17
  48.0 286.9 %collective-permute-start.19 = (bf16[1,1,2,2,1024]{4,3,2,1,0:T(2,128)(2,1)S(1)}, bf16[1,1,2,2,1024]{4,3,2,1,0:T(2,128)(2,1)S(1)}, u32[]{:S(2)}, u32[]{:S(2)}) collective-permute-start(bf16[1,1,2,2,1024]{4,3,2,1,0:T(2,128)(2,1)S(1)} %broadcast_select_fusion.19), channel_id=1, source_target_pairs={{64,0},{80,16},{96,32},{112,48},{128,64},{144,80},{160,96},{176,11... | collective-permute-start | bytes 24584 | tf_op jit(solution)/shard_map/ppermute | solution.py:17
  51.5 288.3 %collective-permute-start.2 = (bf16[1,1,2,2,1024]{4,3,2,1,0:T(2,128)(2,1)S(1)}, bf16[1,1,2,2,1024]{4,3,2,1,0:T(2,128)(2,1)S(1)}, u32[]{:S(2)}, u32[]{:S(2)}) collective-permute-start(bf16[1,1,2,2,1024]{4,3,2,1,0:T(2,128)(2,1)S(1)} %broadcast_select_fusion.28), channel_id=1, source_target_pairs={{64,0},{80,16},{96,32},{112,48},{128,64},{144,80},{160,96},{176,11... | collective-permute-start | bytes 24584 | tf_op jit(solution)/shard_map/ppermute | solution.py:17
  334.9 308.1 %all-gather.3.cloned.1.call-start = ((), (), s32[]{:S(2)}) async-start(), calls=%async_computation | async-start | bytes 4456448 | tf_op jit(solution)/shard_map/all_gather | solution.py:146
  335.0 11.3 %collective-permute-start.20 = (bf16[1,1,2,2,1024]{4,3,2,1,0:T(2,128)(2,1)S(1)}, bf16[1,1,2,2,1024]{4,3,2,1,0:T(2,128)(2,1)S(1)}, u32[]{:S(2)}, u32[]{:S(2)}) collective-permute-start(bf16[1,1,2,2,1024]{4,3,2,1,0:T(2,128)(2,1)S(1)} %broadcast_select_fusion.20), channel_id=1, source_target_pairs={{128,0},{144,16},{160,32},{176,48},{192,64},{208,80},{224,96},{240... | collective-permute-start | bytes 24584 | tf_op jit(solution)/shard_map/ppermute | solution.py:17
  339.8 13.4 %collective-permute-start.3 = (bf16[1,1,2,2,1024]{4,3,2,1,0:T(2,128)(2,1)S(1)}, bf16[1,1,2,2,1024]{4,3,2,1,0:T(2,128)(2,1)S(1)}, u32[]{:S(2)}, u32[]{:S(2)}) collective-permute-start(bf16[1,1,2,2,1024]{4,3,2,1,0:T(2,128)(2,1)S(1)} %broadcast_select_fusion.29), channel_id=1, source_target_pairs={{128,0},{144,16},{160,32},{176,48},{192,64},{208,80},{224,96},{240... | collective-permute-start | bytes 24584 | tf_op jit(solution)/shard_map/ppermute | solution.py:17
  346.3 14.6 %collective-permute-start.21 = (bf16[1,1,2,2,1024]{4,3,2,1,0:T(2,128)(2,1)S(1)}, bf16[1,1,2,2,1024]{4,3,2,1,0:T(2,128)(2,1)S(1)}, u32[]{:S(2)}, u32[]{:S(2)}) collective-permute-start(bf16[1,1,2,2,1024]{4,3,2,1,0:T(2,128)(2,1)S(1)} %broadcast_select_fusion.21), channel_id=1, source_target_pairs={{256,0},{272,16},{288,32},{304,48},{320,64},{336,80},{352,96},{368... | collective-permute-start | bytes 24584 | tf_op jit(solution)/shard_map/ppermute | solution.py:17
  353.3 14.3 %collective-permute-start.4 = (bf16[1,1,2,2,1024]{4,3,2,1,0:T(2,128)(2,1)S(1)}, bf16[1,1,2,2,1024]{4,3,2,1,0:T(2,128)(2,1)S(1)}, u32[]{:S(2)}, u32[]{:S(2)}) collective-permute-start(bf16[1,1,2,2,1024]{4,3,2,1,0:T(2,128)(2,1)S(1)} %broadcast_select_fusion.30), channel_id=1, source_target_pairs={{256,0},{272,16},{288,32},{304,48},{320,64},{336,80},{352,96},{368... | collective-permute-start | bytes 24584 | tf_op jit(solution)/shard_map/ppermute | solution.py:17
  361.0 8.5 %collective-permute-start.22 = (bf16[1,1,2,2,1024]{4,3,2,1,0:T(2,128)(2,1)S(1)}, bf16[1,1,2,2,1024]{4,3,2,1,0:T(2,128)(2,1)S(1)}, u32[]{:S(2)}, u32[]{:S(2)}) collective-permute-start(bf16[1,1,2,2,1024]{4,3,2,1,0:T(2,128)(2,1)S(1)} %broadcast_select_fusion.22), channel_id=1, source_target_pairs={{1,0},{2,1},{3,2},{4,3},{5,4},{6,5},{7,6},{8,7},{9,8},{10,9},{11,1... | collective-permute-start | bytes 24584 | tf_op jit(solution)/shard_map/ppermute | solution.py:17
  369.5 8.1 %collective-permute-start.23 = (bf16[1,1,2,2,1024]{4,3,2,1,0:T(2,128)(2,1)S(1)}, bf16[1,1,2,2,1024]{4,3,2,1,0:T(2,128)(2,1)S(1)}, u32[]{:S(2)}, u32[]{:S(2)}) collective-permute-start(bf16[1,1,2,2,1024]{4,3,2,1,0:T(2,128)(2,1)S(1)} %broadcast_select_fusion.23), channel_id=1, source_target_pairs={{2,0},{3,1},{4,2},{5,3},{6,4},{7,5},{8,6},{9,7},{10,8},{11,9},{12,... | collective-permute-start | bytes 24584 | tf_op jit(solution)/shard_map/ppermute | solution.py:17
  372.3 9.5 %collective-permute-start.6 = (bf16[1,1,2,2,1024]{4,3,2,1,0:T(2,128)(2,1)S(1)}, bf16[1,1,2,2,1024]{4,3,2,1,0:T(2,128)(2,1)S(1)}, u32[]{:S(2)}, u32[]{:S(2)}) collective-permute-start(bf16[1,1,2,2,1024]{4,3,2,1,0:T(2,128)(2,1)S(1)} %broadcast_select_fusion.32), channel_id=1, source_target_pairs={{2,0},{3,1},{4,2},{5,3},{6,4},{7,5},{8,6},{9,7},{10,8},{11,9},{12,... | collective-permute-start | bytes 24584 | tf_op jit(solution)/shard_map/ppermute | solution.py:17
  384.7 7.4 %collective-permute-start.25 = (bf16[1,1,2,2,1024]{4,3,2,1,0:T(2,128)(2,1)S(1)}, bf16[1,1,2,2,1024]{4,3,2,1,0:T(2,128)(2,1)S(1)}, u32[]{:S(2)}, u32[]{:S(2)}) collective-permute-start(bf16[1,1,2,2,1024]{4,3,2,1,0:T(2,128)(2,1)S(1)} %broadcast_select_fusion.25), channel_id=1, source_target_pairs={{8,0},{9,1},{10,2},{11,3},{12,4},{13,5},{14,6},{15,7},{0,8},{1,9},... | collective-permute-start | bytes 24584 | tf_op jit(solution)/shard_map/ppermute | solution.py:17
  392.2 11.1 %collective-permute-start.26 = (bf16[1,1,2,64,1024]{4,3,2,1,0:T(8,128)(2,1)S(1)}, bf16[1,1,2,64,1024]{4,3,2,1,0:T(8,128)(2,1)S(1)}, u32[]{:S(2)}, u32[]{:S(2)}) collective-permute-start(bf16[1,1,2,64,1024]{4,3,2,1,0:T(8,128)(2,1)S(1)} %get-tuple-element.517), channel_id=1, source_target_pairs={{32,0},{48,16},{64,32},{80,48},{96,64},{112,80},{128,96},{144,112}... | collective-permute-start | bytes 786440 | tf_op jit(solution)/shard_map/ppermute | solution.py:17
  394.8 15.7 %collective-permute-start.10 = (bf16[1,1,2,64,1024]{4,3,2,1,0:T(8,128)(2,1)S(1)}, bf16[1,1,2,64,1024]{4,3,2,1,0:T(8,128)(2,1)S(1)}, u32[]{:S(2)}, u32[]{:S(2)}) collective-permute-start(bf16[1,1,2,64,1024]{4,3,2,1,0:T(8,128)(2,1)S(1)} %get-tuple-element.518), channel_id=1, source_target_pairs={{32,0},{48,16},{64,32},{80,48},{96,64},{112,80},{128,96},{144,112}... | collective-permute-start | bytes 786440 | tf_op jit(solution)/shard_map/ppermute | solution.py:17
  403.3 23.4 %collective-permute-start.27 = (bf16[1,1,2,64,1024]{4,3,2,1,0:T(8,128)(2,1)S(1)}, bf16[1,1,2,64,1024]{4,3,2,1,0:T(8,128)(2,1)S(1)}, u32[]{:S(2)}, u32[]{:S(2)}) collective-permute-start(bf16[1,1,2,64,1024]{4,3,2,1,0:T(8,128)(2,1)S(1)} %broadcast_select_fusion.3), channel_id=1, source_target_pairs={{64,0},{80,16},{96,32},{112,48},{128,64},{144,80},{160,96},{176,11... | collective-permute-start | bytes 786440 | tf_op jit(solution)/shard_map/ppermute | solution.py:17
  410.6 49.9 %collective-permute-start.11 = (bf16[1,1,2,64,1024]{4,3,2,1,0:T(8,128)(2,1)S(1)}, bf16[1,1,2,64,1024]{4,3,2,1,0:T(8,128)(2,1)S(1)}, u32[]{:S(2)}, u32[]{:S(2)}) collective-permute-start(bf16[1,1,2,64,1024]{4,3,2,1,0:T(8,128)(2,1)S(1)} %broadcast_select_fusion.11), channel_id=1, source_target_pairs={{64,0},{80,16},{96,32},{112,48},{128,64},{144,80},{160,96},{176,11... | collective-permute-start | bytes 786440 | tf_op jit(solution)/shard_map/ppermute | solution.py:17
  426.8 35.7 %collective-permute-start.28 = (bf16[1,1,2,64,1024]{4,3,2,1,0:T(8,128)(2,1)S(1)}, bf16[1,1,2,64,1024]{4,3,2,1,0:T(8,128)(2,1)S(1)}, u32[]{:S(2)}, u32[]{:S(2)}) collective-permute-start(bf16[1,1,2,64,1024]{4,3,2,1,0:T(8,128)(2,1)S(1)} %broadcast_select_fusion.4), channel_id=1, source_target_pairs={{128,0},{144,16},{160,32},{176,48},{192,64},{208,80},{224,96},{240... | collective-permute-start | bytes 786440 | tf_op jit(solution)/shard_map/ppermute | solution.py:17
  460.5 58.4 %collective-permute-start.12 = (bf16[1,1,2,64,1024]{4,3,2,1,0:T(8,128)(2,1)S(1)}, bf16[1,1,2,64,1024]{4,3,2,1,0:T(8,128)(2,1)S(1)}, u32[]{:S(2)}, u32[]{:S(2)}) collective-permute-start(bf16[1,1,2,64,1024]{4,3,2,1,0:T(8,128)(2,1)S(1)} %broadcast_select_fusion.12), channel_id=1, source_target_pairs={{128,0},{144,16},{160,32},{176,48},{192,64},{208,80},{224,96},{240... | collective-permute-start | bytes 786440 | tf_op jit(solution)/shard_map/ppermute | solution.py:17
  462.5 65.1 %collective-permute-start.29 = (bf16[1,1,2,64,1024]{4,3,2,1,0:T(8,128)(2,1)S(1)}, bf16[1,1,2,64,1024]{4,3,2,1,0:T(8,128)(2,1)S(1)}, u32[]{:S(2)}, u32[]{:S(2)}) collective-permute-start(bf16[1,1,2,64,1024]{4,3,2,1,0:T(8,128)(2,1)S(1)} %broadcast_select_fusion.5), channel_id=1, source_target_pairs={{256,0},{272,16},{288,32},{304,48},{320,64},{336,80},{352,96},{368... | collective-permute-start | bytes 786440 | tf_op jit(solution)/shard_map/ppermute | solution.py:17
  518.9 17.1 %collective-permute-start.13 = (bf16[1,1,2,64,1024]{4,3,2,1,0:T(8,128)(2,1)S(1)}, bf16[1,1,2,64,1024]{4,3,2,1,0:T(8,128)(2,1)S(1)}, u32[]{:S(2)}, u32[]{:S(2)}) collective-permute-start(bf16[1,1,2,64,1024]{4,3,2,1,0:T(8,128)(2,1)S(1)} %broadcast_select_fusion.13), channel_id=1, source_target_pairs={{256,0},{272,16},{288,32},{304,48},{320,64},{336,80},{352,96},{368... | collective-permute-start | bytes 786440 | tf_op jit(solution)/shard_map/ppermute | solution.py:17
  527.7 10.3 %collective-permute-start.30 = (bf16[1,1,2,64,1024]{4,3,2,1,0:T(8,128)(2,1)S(1)}, bf16[1,1,2,64,1024]{4,3,2,1,0:T(8,128)(2,1)S(1)}, u32[]{:S(2)}, u32[]{:S(2)}) collective-permute-start(bf16[1,1,2,64,1024]{4,3,2,1,0:T(8,128)(2,1)S(1)} %broadcast_select_fusion.6), channel_id=1, source_target_pairs={{1,0},{2,1},{3,2},{4,3},{5,4},{6,5},{7,6},{8,7},{9,8},{10,9},{11,1... | collective-permute-start | bytes 786440 | tf_op jit(solution)/shard_map/ppermute | solution.py:17
  538.0 19.7 %collective-permute-start.31 = (bf16[1,1,2,64,1024]{4,3,2,1,0:T(8,128)(2,1)S(1)}, bf16[1,1,2,64,1024]{4,3,2,1,0:T(8,128)(2,1)S(1)}, u32[]{:S(2)}, u32[]{:S(2)}) collective-permute-start(bf16[1,1,2,64,1024]{4,3,2,1,0:T(8,128)(2,1)S(1)} %broadcast_select_fusion.7), channel_id=1, source_target_pairs={{2,0},{3,1},{4,2},{5,3},{6,4},{7,5},{8,6},{9,7},{10,8},{11,9},{12,... | collective-permute-start | bytes 786440 | tf_op jit(solution)/shard_map/ppermute | solution.py:17
  542.9 24.6 %collective-permute-start.15 = (bf16[1,1,2,64,1024]{4,3,2,1,0:T(8,128)(2,1)S(1)}, bf16[1,1,2,64,1024]{4,3,2,1,0:T(8,128)(2,1)S(1)}, u32[]{:S(2)}, u32[]{:S(2)}) collective-permute-start(bf16[1,1,2,64,1024]{4,3,2,1,0:T(8,128)(2,1)S(1)} %broadcast_select_fusion.15), channel_id=1, source_target_pairs={{2,0},{3,1},{4,2},{5,3},{6,4},{7,5},{8,6},{9,7},{10,8},{11,9},{12,... | collective-permute-start | bytes 786440 | tf_op jit(solution)/shard_map/ppermute | solution.py:17
  557.8 15.0 %collective-permute-start.32 = (bf16[1,1,2,64,1024]{4,3,2,1,0:T(8,128)(2,1)S(1)}, bf16[1,1,2,64,1024]{4,3,2,1,0:T(8,128)(2,1)S(1)}, u32[]{:S(2)}, u32[]{:S(2)}) collective-permute-start(bf16[1,1,2,64,1024]{4,3,2,1,0:T(8,128)(2,1)S(1)} %broadcast_select_fusion.8), channel_id=1, source_target_pairs={{4,0},{5,1},{6,2},{7,3},{8,4},{9,5},{10,6},{11,7},{12,8},{13,9},{1... | collective-permute-start | bytes 786440 | tf_op jit(solution)/shard_map/ppermute | solution.py:17
  567.6 19.1 %collective-permute-start.16 = (bf16[1,1,2,64,1024]{4,3,2,1,0:T(8,128)(2,1)S(1)}, bf16[1,1,2,64,1024]{4,3,2,1,0:T(8,128)(2,1)S(1)}, u32[]{:S(2)}, u32[]{:S(2)}) collective-permute-start(bf16[1,1,2,64,1024]{4,3,2,1,0:T(8,128)(2,1)S(1)} %broadcast_select_fusion.16), channel_id=1, source_target_pairs={{4,0},{5,1},{6,2},{7,3},{8,4},{9,5},{10,6},{11,7},{12,8},{13,9},{1... | collective-permute-start | bytes 786440 | tf_op jit(solution)/shard_map/ppermute | solution.py:17
  572.8 15.8 %collective-permute-start.33 = (bf16[1,1,2,64,1024]{4,3,2,1,0:T(8,128)(2,1)S(1)}, bf16[1,1,2,64,1024]{4,3,2,1,0:T(8,128)(2,1)S(1)}, u32[]{:S(2)}, u32[]{:S(2)}) collective-permute-start(bf16[1,1,2,64,1024]{4,3,2,1,0:T(8,128)(2,1)S(1)} %broadcast_select_fusion.9), channel_id=1, source_target_pairs={{8,0},{9,1},{10,2},{11,3},{12,4},{13,5},{14,6},{15,7},{0,8},{1,9},... | collective-permute-start | bytes 786440 | tf_op jit(solution)/shard_map/ppermute | solution.py:17
  586.7 15.3 %collective-permute-start.17 = (bf16[1,1,2,64,1024]{4,3,2,1,0:T(8,128)(2,1)S(1)}, bf16[1,1,2,64,1024]{4,3,2,1,0:T(8,128)(2,1)S(1)}, u32[]{:S(2)}, u32[]{:S(2)}) collective-permute-start(bf16[1,1,2,64,1024]{4,3,2,1,0:T(8,128)(2,1)S(1)} %broadcast_select_fusion.17), channel_id=1, source_target_pairs={{8,0},{9,1},{10,2},{11,3},{12,4},{13,5},{14,6},{15,7},{0,8},{1,9},... | collective-permute-start | bytes 786440 | tf_op jit(solution)/shard_map/ppermute | solution.py:17
  (9 other events, 96.3 us)
Sparse Core Ops, SparseCore 0:
  22.5 312.3 all-reduce.2
  337.0 43.0 all-gather.4
  576.7 41.7 all-gather.2
where the time goes:
time: 692 us; the launch traced here: 690 us
  waiting for transfers between devices  415 us (60%)
  starting transfers between devices  157 us (23%)
  other arithmetic  31.9 us (5%)
  between operations  29.7 us (4%)
  local copies, waits for them, and re-layouts  27.8 us (4%)
  matrix products  27.7 us (4%)
    psum x1, waiting for transfers between devices, spread(): return lax.psum(jnp.where(mine, shard, jnp.zeros_like(shard)), axis)  279 us
    ppermute x34, starting transfers between devices, passed_along(): return lax.ppermute(block, axis, route)  157 us
    ppermute x34, waiting for transfers between devices, passed_along(): return lax.ppermute(block, axis, route)  136 us
    another operation x8, other arithmetic  28.5 us
    while x2, local copies, waits for them, and re-layouts, pair_term(): return lax.map(one_vector, amplitude)  22.5 us
    dot_general x8, matrix products, add_block(): lax.dot_general(left_factor, partner_rows, (((0,), (0,)), ((), ())), pref...  22.4 us
  transfers between devices with their start and end apart: 37, of which 13 were waited for; matrix products, arithmetic and copies ran while one was open for 7% of the time, Pallas kernels for 0%

commit v1 on v0

--- a/solution.py
+++ b/solution.py
@@ -8,7 +8,7 @@
 
 def spread(shard, axis, root):
     mine = lax.axis_index(axis) == root
-    return lax.psum(jnp.where(mine, shard, jnp.zeros_like(shard)), axis)
+    return jnp.sum(lax.all_gather(jnp.where(mine, shard, jnp.zeros_like(shard)), axis), axis=0)
 
 
 def passed_along(block, axis, distance):

time: 692 us -> 588 us (0.85)
  the two profiles are of different devices: /device:TPU:70 before, /device:TPU:1 now
where the time goes in v1:
time: 588 us; the launch traced here: 586 us
  waiting for transfers between devices  267 us (45%)
  starting transfers between devices  186 us (32%)
  other arithmetic  45.5 us (8%)
  between operations  29.7 us (5%)
  local copies, waits for them, and re-layouts  29.4 us (5%)
  matrix products  27.6 us (5%)
    ppermute x34, starting transfers between devices, passed_along(): return lax.ppermute(block, axis, route)  186 us
    all_gather x2, waiting for transfers between devices, spread(): lax.all_gather(jnp.where(mine, shard, jnp.zeros_like(shard)), axis)  122 us
    ppermute x34, waiting for transfers between devices, passed_along(): return lax.ppermute(block, axis, route)  117 us
    another operation x8, other arithmetic  29 us
    all_gather x2, waiting for transfers between devices, shards(): full_screen = lax.all_gather(rows_list[transfer], 'kz', axis=1, tiled=True)  27.1 us
    while x2, local copies, waits for them, and re-layouts, pair_term(): return lax.map(one_vector, amplitude)  22.3 us
    dot_general x8, matrix products, add_block(): lax.dot_general(left_factor, partner_rows, (((0,), (0,)), ((), ())), pref...  22.2 us
  transfers between devices with their start and end apart: 38, of which 16 were waited for; matrix products, arithmetic and copies ran while one was open for 10% of the time, Pallas kernels for 0%

profile of v1, /device:TPU:1, one launch (start us, length us, event | category | flops | bytes accessed | tf_op | source)
XLA Modules:
  0.0 586.4 jit_solution(17249593187681817824)
XLA Ops:
  15.7 14.4 %collective-permute-start.9 = (bf16[1,1,2,64,1024]{4,3,2,1,0:T(8,128)(2,1)}, bf16[1,1,2,64,1024]{4,3,2,1,0:T(8,128)(2,1)S(1)}, u32[]{:S(2)}, u32[]{:S(2)}) collective-permute-start(bf16[1,1,2,64,1024]{4,3,2,1,0:T(8,128)(2,1)} %param.14), channel_id=1, source_target_pairs={{16,0},{32,16},{48,32},{64,48},{80,64},{96,80},{112,96},{128,112},... | collective-permute-start | bytes 786440 | tf_op jit(solution)/shard_map/ppermute | solution.py:17
  67.8 7.8 %collective-permute-start.21 = (bf16[1,1,2,2,1024]{4,3,2,1,0:T(2,128)(2,1)S(1)}, bf16[1,1,2,2,1024]{4,3,2,1,0:T(2,128)(2,1)S(1)}, u32[]{:S(2)}, u32[]{:S(2)}) collective-permute-start(bf16[1,1,2,2,1024]{4,3,2,1,0:T(2,128)(2,1)S(1)} %broadcast_select_fusion.19), channel_id=1, source_target_pairs={{256,0},{272,16},{288,32},{304,48},{320,64},{336,80},{352,96},{368... | collective-permute-start | bytes 24584 | tf_op jit(solution)/shard_map/ppermute | solution.py:17
  75.7 6.1 %collective-permute-start.4 = (bf16[1,1,2,2,1024]{4,3,2,1,0:T(2,128)(2,1)S(1)}, bf16[1,1,2,2,1024]{4,3,2,1,0:T(2,128)(2,1)S(1)}, u32[]{:S(2)}, u32[]{:S(2)}) collective-permute-start(bf16[1,1,2,2,1024]{4,3,2,1,0:T(2,128)(2,1)S(1)} %broadcast_select_fusion.28), channel_id=1, source_target_pairs={{256,0},{272,16},{288,32},{304,48},{320,64},{336,80},{352,96},{368... | collective-permute-start | bytes 24584 | tf_op jit(solution)/shard_map/ppermute | solution.py:17
  81.8 122.3 %all-gather.9.cloned.1.call-done = bf16[32,2,64,1024]{3,2,1,0:T(8,128)(2,1)} async-done(((bf16[1,2,64,1024]{3,2,1,0:T(8,128)(2,1)}), bf16[32,2,64,1024]{3,2,1,0:T(8,128)(2,1)}) %all-gather.9.cloned.1.call-update) | async-done | bytes 8388624 | tf_op jit(solution)/shard_map/all_gather | solution.py:11
  204.1 5.6 reduce_sum.25
  210.8 10.5 %collective-permute-start.22 = (bf16[1,1,2,2,1024]{4,3,2,1,0:T(2,128)(2,1)S(1)}, bf16[1,1,2,2,1024]{4,3,2,1,0:T(2,128)(2,1)S(1)}, u32[]{:S(2)}, u32[]{:S(2)}) collective-permute-start(bf16[1,1,2,2,1024]{4,3,2,1,0:T(2,128)(2,1)S(1)} %broadcast_select_fusion.20), channel_id=1, source_target_pairs={{1,0},{2,1},{3,2},{4,3},{5,4},{6,5},{7,6},{8,7},{9,8},{10,9},{11,1... | collective-permute-start | bytes 24584 | tf_op jit(solution)/shard_map/ppermute | solution.py:17
  252.5 4.9 collective-permute-done.26
  261.2 5.9 %collective-permute-done.10 = bf16[1,1,2,64,1024]{4,3,2,1,0:T(8,128)(2,1)S(1)} collective-permute-done((bf16[1,1,2,64,1024]{4,3,2,1,0:T(8,128)(2,1)S(1)}, bf16[1,1,2,64,1024]{4,3,2,1,0:T(8,128)(2,1)S(1)}, u32[]{:S(2)}, u32[]{:S(2)}) %collective-permute-start.10) | collective-permute-done | bytes 262176 | tf_op jit(solution)/shard_map/ppermute | solution.py:17
  271.0 12.5 %collective-permute-done.27 = bf16[1,1,2,64,1024]{4,3,2,1,0:T(8,128)(2,1)S(1)} collective-permute-done((bf16[1,1,2,64,1024]{4,3,2,1,0:T(8,128)(2,1)S(1)}, bf16[1,1,2,64,1024]{4,3,2,1,0:T(8,128)(2,1)S(1)}, u32[]{:S(2)}, u32[]{:S(2)}) %collective-permute-start.27) | collective-permute-done | bytes 262176 | tf_op jit(solution)/shard_map/ppermute | solution.py:17
  283.5 10.5 %collective-permute-start.28 = (bf16[1,1,2,64,1024]{4,3,2,1,0:T(8,128)(2,1)S(1)}, bf16[1,1,2,64,1024]{4,3,2,1,0:T(8,128)(2,1)S(1)}, u32[]{:S(2)}, u32[]{:S(2)}) collective-permute-start(bf16[1,1,2,64,1024]{4,3,2,1,0:T(8,128)(2,1)S(1)} %broadcast_select_fusion.2), channel_id=1, source_target_pairs={{128,0},{144,16},{160,32},{176,48},{192,64},{208,80},{224,96},{240... | collective-permute-start | bytes 786440 | tf_op jit(solution)/shard_map/ppermute | solution.py:17
  294.2 15.0 %collective-permute-done.11 = bf16[1,1,2,64,1024]{4,3,2,1,0:T(8,128)(2,1)S(1)} collective-permute-done((bf16[1,1,2,64,1024]{4,3,2,1,0:T(8,128)(2,1)S(1)}, bf16[1,1,2,64,1024]{4,3,2,1,0:T(8,128)(2,1)S(1)}, u32[]{:S(2)}, u32[]{:S(2)}) %collective-permute-start.11) | collective-permute-done | bytes 262176 | tf_op jit(solution)/shard_map/ppermute | solution.py:17
  309.2 7.4 %collective-permute-start.12 = (bf16[1,1,2,64,1024]{4,3,2,1,0:T(8,128)(2,1)S(1)}, bf16[1,1,2,64,1024]{4,3,2,1,0:T(8,128)(2,1)S(1)}, u32[]{:S(2)}, u32[]{:S(2)}) collective-permute-start(bf16[1,1,2,64,1024]{4,3,2,1,0:T(8,128)(2,1)S(1)} %broadcast_select_fusion.10), channel_id=1, source_target_pairs={{128,0},{144,16},{160,32},{176,48},{192,64},{208,80},{224,96},{240... | collective-permute-start | bytes 786440 | tf_op jit(solution)/shard_map/ppermute | solution.py:17
  316.6 34.4 %collective-permute-done.28 = bf16[1,1,2,64,1024]{4,3,2,1,0:T(8,128)(2,1)S(1)} collective-permute-done((bf16[1,1,2,64,1024]{4,3,2,1,0:T(8,128)(2,1)S(1)}, bf16[1,1,2,64,1024]{4,3,2,1,0:T(8,128)(2,1)S(1)}, u32[]{:S(2)}, u32[]{:S(2)}) %collective-permute-start.28) | collective-permute-done | bytes 262176 | tf_op jit(solution)/shard_map/ppermute | solution.py:17
  351.0 10.7 %collective-permute-start.29 = (bf16[1,1,2,64,1024]{4,3,2,1,0:T(8,128)(2,1)S(1)}, bf16[1,1,2,64,1024]{4,3,2,1,0:T(8,128)(2,1)S(1)}, u32[]{:S(2)}, u32[]{:S(2)}) collective-permute-start(bf16[1,1,2,64,1024]{4,3,2,1,0:T(8,128)(2,1)S(1)} %broadcast_select_fusion.3), channel_id=1, source_target_pairs={{256,0},{272,16},{288,32},{304,48},{320,64},{336,80},{352,96},{368... | collective-permute-start | bytes 786440 | tf_op jit(solution)/shard_map/ppermute | solution.py:17
  361.8 29.8 %collective-permute-done.12 = bf16[1,1,2,64,1024]{4,3,2,1,0:T(8,128)(2,1)S(1)} collective-permute-done((bf16[1,1,2,64,1024]{4,3,2,1,0:T(8,128)(2,1)S(1)}, bf16[1,1,2,64,1024]{4,3,2,1,0:T(8,128)(2,1)S(1)}, u32[]{:S(2)}, u32[]{:S(2)}) %collective-permute-start.12) | collective-permute-done | bytes 262176 | tf_op jit(solution)/shard_map/ppermute | solution.py:17
  391.6 9.7 %collective-permute-start.13 = (bf16[1,1,2,64,1024]{4,3,2,1,0:T(8,128)(2,1)S(1)}, bf16[1,1,2,64,1024]{4,3,2,1,0:T(8,128)(2,1)S(1)}, u32[]{:S(2)}, u32[]{:S(2)}) collective-permute-start(bf16[1,1,2,64,1024]{4,3,2,1,0:T(8,128)(2,1)S(1)} %broadcast_select_fusion.11), channel_id=1, source_target_pairs={{256,0},{272,16},{288,32},{304,48},{320,64},{336,80},{352,96},{368... | collective-permute-start | bytes 786440 | tf_op jit(solution)/shard_map/ppermute | solution.py:17
  401.3 6.8 %collective-permute-start.30 = (bf16[1,1,2,64,1024]{4,3,2,1,0:T(8,128)(2,1)S(1)}, bf16[1,1,2,64,1024]{4,3,2,1,0:T(8,128)(2,1)S(1)}, u32[]{:S(2)}, u32[]{:S(2)}) collective-permute-start(bf16[1,1,2,64,1024]{4,3,2,1,0:T(8,128)(2,1)S(1)} %broadcast_select_fusion.4), channel_id=1, source_target_pairs={{1,0},{2,1},{3,2},{4,3},{5,4},{6,5},{7,6},{8,7},{9,8},{10,9},{11,1... | collective-permute-start | bytes 786440 | tf_op jit(solution)/shard_map/ppermute | solution.py:17
  410.4 10.2 %collective-permute-start.14 = (bf16[1,1,2,64,1024]{4,3,2,1,0:T(8,128)(2,1)S(1)}, bf16[1,1,2,64,1024]{4,3,2,1,0:T(8,128)(2,1)S(1)}, u32[]{:S(2)}, u32[]{:S(2)}) collective-permute-start(bf16[1,1,2,64,1024]{4,3,2,1,0:T(8,128)(2,1)S(1)} %broadcast_select_fusion.12), channel_id=1, source_target_pairs={{1,0},{2,1},{3,2},{4,3},{5,4},{6,5},{7,6},{8,7},{9,8},{10,9},{11,1... | collective-permute-start | bytes 786440 | tf_op jit(solution)/shard_map/ppermute | solution.py:17
  420.6 7.6 %collective-permute-start.31 = (bf16[1,1,2,64,1024]{4,3,2,1,0:T(8,128)(2,1)S(1)}, bf16[1,1,2,64,1024]{4,3,2,1,0:T(8,128)(2,1)S(1)}, u32[]{:S(2)}, u32[]{:S(2)}) collective-permute-start(bf16[1,1,2,64,1024]{4,3,2,1,0:T(8,128)(2,1)S(1)} %broadcast_select_fusion.5), channel_id=1, source_target_pairs={{2,0},{3,1},{4,2},{5,3},{6,4},{7,5},{8,6},{9,7},{10,8},{11,9},{12,... | collective-permute-start | bytes 786440 | tf_op jit(solution)/shard_map/ppermute | solution.py:17
  429.9 7.8 %collective-permute-start.15 = (bf16[1,1,2,64,1024]{4,3,2,1,0:T(8,128)(2,1)S(1)}, bf16[1,1,2,64,1024]{4,3,2,1,0:T(8,128)(2,1)S(1)}, u32[]{:S(2)}, u32[]{:S(2)}) collective-permute-start(bf16[1,1,2,64,1024]{4,3,2,1,0:T(8,128)(2,1)S(1)} %broadcast_select_fusion.13), channel_id=1, source_target_pairs={{2,0},{3,1},{4,2},{5,3},{6,4},{7,5},{8,6},{9,7},{10,8},{11,9},{12,... | collective-permute-start | bytes 786440 | tf_op jit(solution)/shard_map/ppermute | solution.py:17
  437.8 6.6 %collective-permute-start.32 = (bf16[1,1,2,64,1024]{4,3,2,1,0:T(8,128)(2,1)S(1)}, bf16[1,1,2,64,1024]{4,3,2,1,0:T(8,128)(2,1)S(1)}, u32[]{:S(2)}, u32[]{:S(2)}) collective-permute-start(bf16[1,1,2,64,1024]{4,3,2,1,0:T(8,128)(2,1)S(1)} %broadcast_select_fusion.6), channel_id=1, source_target_pairs={{4,0},{5,1},{6,2},{7,3},{8,4},{9,5},{10,6},{11,7},{12,8},{13,9},{1... | collective-permute-start | bytes 786440 | tf_op jit(solution)/shard_map/ppermute | solution.py:17
  444.5 5.5 collective-permute-start.16
  464.3 5.6 reduce_sum.24
  471.4 24.0 %all-gather.11.cloned.1.call-done = bf16[2,1024,1024]{2,0,1:T(2,128)(2,1)} async-done(((bf16[2,64,1024]{2,0,1:T(2,128)(2,1)}), bf16[2,1024,1024]{2,0,1:T(2,128)(2,1)}) %all-gather.11.cloned.1.call-update) | async-done | bytes 4194320 | tf_op jit(solution)/shard_map/all_gather | solution.py:146
  495.4 11.2 %copy.24 = bf16[2,1024,1024]{1,2,0:T(8,128)(2,1)} copy(bf16[2,1024,1024]{2,0,1:T(2,128)(2,1)} %all-gather.11.cloned.1.call-done) | data formatting | bytes 8388608 | tf_op jit(solution)/shard_map/while | solution.py:108
  506.6 29.5 %while.51 = (s32[]{:T(128)}, f32[2,2,1024]{2,1,0:T(2,128)S(1)}, bf16[2,2,32,1024]{3,2,1,0:T(8,128)(2,1)S(1)}, bf16[2,32,1024]{2,1,0:T(8,128)(2,1)S(1)}, bf16[2,1...) while((s32[]{:T(128)}, f32[2,2,1024]{2,1,0:T(2,128)S(1)}, ...), condition=%wide.region_9.10_spmd, body=%wide.region_6.9_spmd.sunk | while | flops 283219968 | bytes 16187882 | solution.py:108
  506.6 14.5 %while.53 = (s32[]{:T(128)}, f32[32,64]{1,0:T(8,128)S(1)}, bf16[2,32,1024]{2,1,0:T(8,128)(2,1)S(1)}, bf16[2,1024,1024]{1,2,0:T(8,128)(2,1)}, bf16[32,1024]{1,0:T...) while((s32[]{:T(128)}, f32[32,64]{1,0:T(8,128)S(1)}, ...), condition=%wide.region_8.8_spmd.clone, body=%wide.region_7.7_spmd.clone.sunk | while | flops 283217920 | bytes 15876309 | solution.py:98
  521.4 14.4 %while.53 = (s32[]{:T(128)}, f32[32,64]{1,0:T(8,128)S(1)}, bf16[2,32,1024]{2,1,0:T(8,128)(2,1)S(1)}, bf16[2,1024,1024]{1,2,0:T(8,128)(2,1)}, bf16[32,1024]{1,0:T...) while((s32[]{:T(128)}, f32[32,64]{1,0:T(8,128)S(1)}, ...), condition=%wide.region_8.8_spmd.clone, body=%wide.region_7.7_spmd.clone.sunk | while | flops 283217920 | bytes 15876309 | solution.py:98
  539.3 11.2 %copy.19 = bf16[2,1024,1024]{1,2,0:T(8,128)(2,1)} copy(bf16[2,1024,1024]{2,0,1:T(2,128)(2,1)} %all-gather.7.cloned.1.call-done) | data formatting | bytes 8388608 | tf_op jit(solution)/shard_map/while | solution.py:108
  550.4 28.8 %while.49 = (s32[]{:T(128)}, f32[2,2,1024]{2,1,0:T(2,128)S(1)}, bf16[2,2,32,1024]{3,2,1,0:T(8,128)(2,1)S(1)}, bf16[2,32,1024]{2,1,0:T(8,128)(2,1)S(1)}, bf16[2,1...) while((s32[]{:T(128)}, f32[2,2,1024]{2,1,0:T(2,128)S(1)}, ...), condition=%wide.region_4.5_spmd, body=%wide.region_1.4_spmd.sunk | while | flops 283219968 | bytes 16187882 | solution.py:108
  550.5 14.1 %while.52 = (s32[]{:T(128)}, f32[32,64]{1,0:T(8,128)S(1)}, bf16[2,32,1024]{2,1,0:T(8,128)(2,1)S(1)}, bf16[2,1024,1024]{1,2,0:T(8,128)(2,1)}, bf16[32,1024]{1,0:T...) while((s32[]{:T(128)}, f32[32,64]{1,0:T(8,128)S(1)}, ...), condition=%wide.region_3.3_spmd.clone, body=%wide.region_2.2_spmd.clone.sunk | while | flops 283217920 | bytes 15876309 | solution.py:98
  564.9 14.1 %while.52 = (s32[]{:T(128)}, f32[32,64]{1,0:T(8,128)S(1)}, bf16[2,32,1024]{2,1,0:T(8,128)(2,1)S(1)}, bf16[2,1024,1024]{1,2,0:T(8,128)(2,1)}, bf16[32,1024]{1,0:T...) while((s32[]{:T(128)}, f32[32,64]{1,0:T(8,128)S(1)}, ...), condition=%wide.region_3.3_spmd.clone, body=%wide.region_2.2_spmd.clone.sunk | while | flops 283217920 | bytes 15876309 | solution.py:98
  (208 shorter events, 152.1 us)
Async XLA Ops:
  6.5 197.6 %all-gather.9.cloned.1.call-start = ((), (), s32[]{:S(2)}) async-start(), calls=%async_computation.2 | async-start | bytes 8650752 | tf_op jit(solution)/shard_map/all_gather | solution.py:11
  14.9 449.4 %all-gather.5.cloned.1.call-start = ((), (), s32[]{:S(2)}) async-start(), calls=%async_computation | async-start | bytes 8650752 | tf_op jit(solution)/shard_map/all_gather | solution.py:11
  15.6 479.8 %all-gather.11.cloned.1.call-start = ((), (), s32[]{:S(2)}) async-start(), calls=%async_computation.3 | async-start | bytes 4456448 | tf_op jit(solution)/shard_map/all_gather | solution.py:146
  15.7 228.9 %collective-permute-start.9 = (bf16[1,1,2,64,1024]{4,3,2,1,0:T(8,128)(2,1)}, bf16[1,1,2,64,1024]{4,3,2,1,0:T(8,128)(2,1)S(1)}, u32[]{:S(2)}, u32[]{:S(2)}) collective-permute-start(bf16[1,1,2,64,1024]{4,3,2,1,0:T(8,128)(2,1)} %param.14), channel_id=1, source_target_pairs={{16,0},{32,16},{48,32},{64,48},{80,64},{96,80},{112,96},{128,112},... | collective-permute-start | bytes 786440 | tf_op jit(solution)/shard_map/ppermute | solution.py:17
  30.1 13.4 %collective-permute-start = (bf16[1,1,2,2,1024]{4,3,2,1,0:T(2,128)(2,1)}, bf16[1,1,2,2,1024]{4,3,2,1,0:T(2,128)(2,1)S(1)}, u32[]{:S(2)}, u32[]{:S(2)}) collective-permute-start(bf16[1,1,2,2,1024]{4,3,2,1,0:T(2,128)(2,1)} %param.15), channel_id=1, source_target_pairs={{16,0},{32,16},{48,32},{64,48},{80,64},{96,80},{112,96},{128,112},... | collective-permute-start | bytes 24584 | tf_op jit(solution)/shard_map/ppermute | solution.py:17
  43.6 8.3 %collective-permute-start.18 = (bf16[1,1,2,2,1024]{4,3,2,1,0:T(2,128)(2,1)S(1)}, bf16[1,1,2,2,1024]{4,3,2,1,0:T(2,128)(2,1)S(1)}, u32[]{:S(2)}, u32[]{:S(2)}) collective-permute-start(bf16[1,1,2,2,1024]{4,3,2,1,0:T(2,128)(2,1)S(1)} %get-tuple-element.529), channel_id=1, source_target_pairs={{32,0},{48,16},{64,32},{80,48},{96,64},{112,80},{128,96},{144,112}... | collective-permute-start | bytes 24584 | tf_op jit(solution)/shard_map/ppermute | solution.py:17
  51.9 7.4 %collective-permute-start.19 = (bf16[1,1,2,2,1024]{4,3,2,1,0:T(2,128)(2,1)S(1)}, bf16[1,1,2,2,1024]{4,3,2,1,0:T(2,128)(2,1)S(1)}, u32[]{:S(2)}, u32[]{:S(2)}) collective-permute-start(bf16[1,1,2,2,1024]{4,3,2,1,0:T(2,128)(2,1)S(1)} %broadcast_select_fusion.17), channel_id=1, source_target_pairs={{64,0},{80,16},{96,32},{112,48},{128,64},{144,80},{160,96},{176,11... | collective-permute-start | bytes 24584 | tf_op jit(solution)/shard_map/ppermute | solution.py:17
  59.4 8.4 %collective-permute-start.20 = (bf16[1,1,2,2,1024]{4,3,2,1,0:T(2,128)(2,1)S(1)}, bf16[1,1,2,2,1024]{4,3,2,1,0:T(2,128)(2,1)S(1)}, u32[]{:S(2)}, u32[]{:S(2)}) collective-permute-start(bf16[1,1,2,2,1024]{4,3,2,1,0:T(2,128)(2,1)S(1)} %broadcast_select_fusion.18), channel_id=1, source_target_pairs={{128,0},{144,16},{160,32},{176,48},{192,64},{208,80},{224,96},{240... | collective-permute-start | bytes 24584 | tf_op jit(solution)/shard_map/ppermute | solution.py:17
  62.8 12.9 %collective-permute-start.3 = (bf16[1,1,2,2,1024]{4,3,2,1,0:T(2,128)(2,1)S(1)}, bf16[1,1,2,2,1024]{4,3,2,1,0:T(2,128)(2,1)S(1)}, u32[]{:S(2)}, u32[]{:S(2)}) collective-permute-start(bf16[1,1,2,2,1024]{4,3,2,1,0:T(2,128)(2,1)S(1)} %broadcast_select_fusion.27), channel_id=1, source_target_pairs={{128,0},{144,16},{160,32},{176,48},{192,64},{208,80},{224,96},{240... | collective-permute-start | bytes 24584 | tf_op jit(solution)/shard_map/ppermute | solution.py:17
  67.8 142.9 %collective-permute-start.21 = (bf16[1,1,2,2,1024]{4,3,2,1,0:T(2,128)(2,1)S(1)}, bf16[1,1,2,2,1024]{4,3,2,1,0:T(2,128)(2,1)S(1)}, u32[]{:S(2)}, u32[]{:S(2)}) collective-permute-start(bf16[1,1,2,2,1024]{4,3,2,1,0:T(2,128)(2,1)S(1)} %broadcast_select_fusion.19), channel_id=1, source_target_pairs={{256,0},{272,16},{288,32},{304,48},{320,64},{336,80},{352,96},{368... | collective-permute-start | bytes 24584 | tf_op jit(solution)/shard_map/ppermute | solution.py:17
  75.7 145.6 %collective-permute-start.4 = (bf16[1,1,2,2,1024]{4,3,2,1,0:T(2,128)(2,1)S(1)}, bf16[1,1,2,2,1024]{4,3,2,1,0:T(2,128)(2,1)S(1)}, u32[]{:S(2)}, u32[]{:S(2)}) collective-permute-start(bf16[1,1,2,2,1024]{4,3,2,1,0:T(2,128)(2,1)S(1)} %broadcast_select_fusion.28), channel_id=1, source_target_pairs={{256,0},{272,16},{288,32},{304,48},{320,64},{336,80},{352,96},{368... | collective-permute-start | bytes 24584 | tf_op jit(solution)/shard_map/ppermute | solution.py:17
  210.7 328.6 %all-gather.7.cloned.1.call-start = ((), (), s32[]{:S(2)}) async-start(), calls=%async_computation.1 | async-start | bytes 4456448 | tf_op jit(solution)/shard_map/all_gather | solution.py:146
  210.8 12.4 %collective-permute-start.22 = (bf16[1,1,2,2,1024]{4,3,2,1,0:T(2,128)(2,1)S(1)}, bf16[1,1,2,2,1024]{4,3,2,1,0:T(2,128)(2,1)S(1)}, u32[]{:S(2)}, u32[]{:S(2)}) collective-permute-start(bf16[1,1,2,2,1024]{4,3,2,1,0:T(2,128)(2,1)S(1)} %broadcast_select_fusion.20), channel_id=1, source_target_pairs={{1,0},{2,1},{3,2},{4,3},{5,4},{6,5},{7,6},{8,7},{9,8},{10,9},{11,1... | collective-permute-start | bytes 24584 | tf_op jit(solution)/shard_map/ppermute | solution.py:17
  223.2 9.6 %collective-permute-start.23 = (bf16[1,1,2,2,1024]{4,3,2,1,0:T(2,128)(2,1)S(1)}, bf16[1,1,2,2,1024]{4,3,2,1,0:T(2,128)(2,1)S(1)}, u32[]{:S(2)}, u32[]{:S(2)}) collective-permute-start(bf16[1,1,2,2,1024]{4,3,2,1,0:T(2,128)(2,1)S(1)} %broadcast_select_fusion.21), channel_id=1, source_target_pairs={{2,0},{3,1},{4,2},{5,3},{6,4},{7,5},{8,6},{9,7},{10,8},{11,9},{12,... | collective-permute-start | bytes 24584 | tf_op jit(solution)/shard_map/ppermute | solution.py:17
  234.8 7.1 %collective-permute-start.7 = (bf16[1,1,2,2,1024]{4,3,2,1,0:T(2,128)(2,1)S(1)}, bf16[1,1,2,2,1024]{4,3,2,1,0:T(2,128)(2,1)S(1)}, u32[]{:S(2)}, u32[]{:S(2)}) collective-permute-start(bf16[1,1,2,2,1024]{4,3,2,1,0:T(2,128)(2,1)S(1)} %broadcast_select_fusion.31), channel_id=1, source_target_pairs={{4,0},{5,1},{6,2},{7,3},{8,4},{9,5},{10,6},{11,7},{12,8},{13,9},{1... | collective-permute-start | bytes 24584 | tf_op jit(solution)/shard_map/ppermute | solution.py:17
  241.9 7.2 %collective-permute-start.8 = (bf16[1,1,2,2,1024]{4,3,2,1,0:T(2,128)(2,1)S(1)}, bf16[1,1,2,2,1024]{4,3,2,1,0:T(2,128)(2,1)S(1)}, u32[]{:S(2)}, u32[]{:S(2)}) collective-permute-start(bf16[1,1,2,2,1024]{4,3,2,1,0:T(2,128)(2,1)S(1)} %broadcast_select_fusion.32), channel_id=1, source_target_pairs={{8,0},{9,1},{10,2},{11,3},{12,4},{13,5},{14,6},{15,7},{0,8},{1,9},... | collective-permute-start | bytes 24584 | tf_op jit(solution)/shard_map/ppermute | solution.py:17
  244.6 12.8 %collective-permute-start.26 = (bf16[1,1,2,64,1024]{4,3,2,1,0:T(8,128)(2,1)S(1)}, bf16[1,1,2,64,1024]{4,3,2,1,0:T(8,128)(2,1)S(1)}, u32[]{:S(2)}, u32[]{:S(2)}) collective-permute-start(bf16[1,1,2,64,1024]{4,3,2,1,0:T(8,128)(2,1)S(1)} %get-tuple-element.515), channel_id=1, source_target_pairs={{32,0},{48,16},{64,32},{80,48},{96,64},{112,80},{128,96},{144,112}... | collective-permute-start | bytes 786440 | tf_op jit(solution)/shard_map/ppermute | solution.py:17
  249.3 17.8 %collective-permute-start.10 = (bf16[1,1,2,64,1024]{4,3,2,1,0:T(8,128)(2,1)S(1)}, bf16[1,1,2,64,1024]{4,3,2,1,0:T(8,128)(2,1)S(1)}, u32[]{:S(2)}, u32[]{:S(2)}) collective-permute-start(bf16[1,1,2,64,1024]{4,3,2,1,0:T(8,128)(2,1)S(1)} %get-tuple-element.516), channel_id=1, source_target_pairs={{32,0},{48,16},{64,32},{80,48},{96,64},{112,80},{128,96},{144,112}... | collective-permute-start | bytes 786440 | tf_op jit(solution)/shard_map/ppermute | solution.py:17
  257.5 26.0 %collective-permute-start.27 = (bf16[1,1,2,64,1024]{4,3,2,1,0:T(8,128)(2,1)S(1)}, bf16[1,1,2,64,1024]{4,3,2,1,0:T(8,128)(2,1)S(1)}, u32[]{:S(2)}, u32[]{:S(2)}) collective-permute-start(bf16[1,1,2,64,1024]{4,3,2,1,0:T(8,128)(2,1)S(1)} %broadcast_select_fusion.1), channel_id=1, source_target_pairs={{64,0},{80,16},{96,32},{112,48},{128,64},{144,80},{160,96},{176,11... | collective-permute-start | bytes 786440 | tf_op jit(solution)/shard_map/ppermute | solution.py:17
  267.2 42.0 %collective-permute-start.11 = (bf16[1,1,2,64,1024]{4,3,2,1,0:T(8,128)(2,1)S(1)}, bf16[1,1,2,64,1024]{4,3,2,1,0:T(8,128)(2,1)S(1)}, u32[]{:S(2)}, u32[]{:S(2)}) collective-permute-start(bf16[1,1,2,64,1024]{4,3,2,1,0:T(8,128)(2,1)S(1)} %broadcast_select_fusion.9), channel_id=1, source_target_pairs={{64,0},{80,16},{96,32},{112,48},{128,64},{144,80},{160,96},{176,11... | collective-permute-start | bytes 786440 | tf_op jit(solution)/shard_map/ppermute | solution.py:17
  283.5 67.4 %collective-permute-start.28 = (bf16[1,1,2,64,1024]{4,3,2,1,0:T(8,128)(2,1)S(1)}, bf16[1,1,2,64,1024]{4,3,2,1,0:T(8,128)(2,1)S(1)}, u32[]{:S(2)}, u32[]{:S(2)}) collective-permute-start(bf16[1,1,2,64,1024]{4,3,2,1,0:T(8,128)(2,1)S(1)} %broadcast_select_fusion.2), channel_id=1, source_target_pairs={{128,0},{144,16},{160,32},{176,48},{192,64},{208,80},{224,96},{240... | collective-permute-start | bytes 786440 | tf_op jit(solution)/shard_map/ppermute | solution.py:17
  309.2 82.4 %collective-permute-start.12 = (bf16[1,1,2,64,1024]{4,3,2,1,0:T(8,128)(2,1)S(1)}, bf16[1,1,2,64,1024]{4,3,2,1,0:T(8,128)(2,1)S(1)}, u32[]{:S(2)}, u32[]{:S(2)}) collective-permute-start(bf16[1,1,2,64,1024]{4,3,2,1,0:T(8,128)(2,1)S(1)} %broadcast_select_fusion.10), channel_id=1, source_target_pairs={{128,0},{144,16},{160,32},{176,48},{192,64},{208,80},{224,96},{240... | collective-permute-start | bytes 786440 | tf_op jit(solution)/shard_map/ppermute | solution.py:17
  351.0 50.3 %collective-permute-start.29 = (bf16[1,1,2,64,1024]{4,3,2,1,0:T(8,128)(2,1)S(1)}, bf16[1,1,2,64,1024]{4,3,2,1,0:T(8,128)(2,1)S(1)}, u32[]{:S(2)}, u32[]{:S(2)}) collective-permute-start(bf16[1,1,2,64,1024]{4,3,2,1,0:T(8,128)(2,1)S(1)} %broadcast_select_fusion.3), channel_id=1, source_target_pairs={{256,0},{272,16},{288,32},{304,48},{320,64},{336,80},{352,96},{368... | collective-permute-start | bytes 786440 | tf_op jit(solution)/shard_map/ppermute | solution.py:17
  391.6 18.7 %collective-permute-start.13 = (bf16[1,1,2,64,1024]{4,3,2,1,0:T(8,128)(2,1)S(1)}, bf16[1,1,2,64,1024]{4,3,2,1,0:T(8,128)(2,1)S(1)}, u32[]{:S(2)}, u32[]{:S(2)}) collective-permute-start(bf16[1,1,2,64,1024]{4,3,2,1,0:T(8,128)(2,1)S(1)} %broadcast_select_fusion.11), channel_id=1, source_target_pairs={{256,0},{272,16},{288,32},{304,48},{320,64},{336,80},{352,96},{368... | collective-permute-start | bytes 786440 | tf_op jit(solution)/shard_map/ppermute | solution.py:17
  401.3 19.2 %collective-permute-start.30 = (bf16[1,1,2,64,1024]{4,3,2,1,0:T(8,128)(2,1)S(1)}, bf16[1,1,2,64,1024]{4,3,2,1,0:T(8,128)(2,1)S(1)}, u32[]{:S(2)}, u32[]{:S(2)}) collective-permute-start(bf16[1,1,2,64,1024]{4,3,2,1,0:T(8,128)(2,1)S(1)} %broadcast_select_fusion.4), channel_id=1, source_target_pairs={{1,0},{2,1},{3,2},{4,3},{5,4},{6,5},{7,6},{8,7},{9,8},{10,9},{11,1... | collective-permute-start | bytes 786440 | tf_op jit(solution)/shard_map/ppermute | solution.py:17
  410.4 19.5 %collective-permute-start.14 = (bf16[1,1,2,64,1024]{4,3,2,1,0:T(8,128)(2,1)S(1)}, bf16[1,1,2,64,1024]{4,3,2,1,0:T(8,128)(2,1)S(1)}, u32[]{:S(2)}, u32[]{:S(2)}) collective-permute-start(bf16[1,1,2,64,1024]{4,3,2,1,0:T(8,128)(2,1)S(1)} %broadcast_select_fusion.12), channel_id=1, source_target_pairs={{1,0},{2,1},{3,2},{4,3},{5,4},{6,5},{7,6},{8,7},{9,8},{10,9},{11,1... | collective-permute-start | bytes 786440 | tf_op jit(solution)/shard_map/ppermute | solution.py:17
  420.6 17.1 %collective-permute-start.31 = (bf16[1,1,2,64,1024]{4,3,2,1,0:T(8,128)(2,1)S(1)}, bf16[1,1,2,64,1024]{4,3,2,1,0:T(8,128)(2,1)S(1)}, u32[]{:S(2)}, u32[]{:S(2)}) collective-permute-start(bf16[1,1,2,64,1024]{4,3,2,1,0:T(8,128)(2,1)S(1)} %broadcast_select_fusion.5), channel_id=1, source_target_pairs={{2,0},{3,1},{4,2},{5,3},{6,4},{7,5},{8,6},{9,7},{10,8},{11,9},{12,... | collective-permute-start | bytes 786440 | tf_op jit(solution)/shard_map/ppermute | solution.py:17
  429.9 14.6 %collective-permute-start.15 = (bf16[1,1,2,64,1024]{4,3,2,1,0:T(8,128)(2,1)S(1)}, bf16[1,1,2,64,1024]{4,3,2,1,0:T(8,128)(2,1)S(1)}, u32[]{:S(2)}, u32[]{:S(2)}) collective-permute-start(bf16[1,1,2,64,1024]{4,3,2,1,0:T(8,128)(2,1)S(1)} %broadcast_select_fusion.13), channel_id=1, source_target_pairs={{2,0},{3,1},{4,2},{5,3},{6,4},{7,5},{8,6},{9,7},{10,8},{11,9},{12,... | collective-permute-start | bytes 786440 | tf_op jit(solution)/shard_map/ppermute | solution.py:17
  437.8 12.2 %collective-permute-start.32 = (bf16[1,1,2,64,1024]{4,3,2,1,0:T(8,128)(2,1)S(1)}, bf16[1,1,2,64,1024]{4,3,2,1,0:T(8,128)(2,1)S(1)}, u32[]{:S(2)}, u32[]{:S(2)}) collective-permute-start(bf16[1,1,2,64,1024]{4,3,2,1,0:T(8,128)(2,1)S(1)} %broadcast_select_fusion.6), channel_id=1, source_target_pairs={{4,0},{5,1},{6,2},{7,3},{8,4},{9,5},{10,6},{11,7},{12,8},{13,9},{1... | collective-permute-start | bytes 786440 | tf_op jit(solution)/shard_map/ppermute | solution.py:17
  444.5 10.5 %collective-permute-start.16 = (bf16[1,1,2,64,1024]{4,3,2,1,0:T(8,128)(2,1)S(1)}, bf16[1,1,2,64,1024]{4,3,2,1,0:T(8,128)(2,1)S(1)}, u32[]{:S(2)}, u32[]{:S(2)}) collective-permute-start(bf16[1,1,2,64,1024]{4,3,2,1,0:T(8,128)(2,1)S(1)} %broadcast_select_fusion.14), channel_id=1, source_target_pairs={{4,0},{5,1},{6,2},{7,3},{8,4},{9,5},{10,6},{11,7},{12,8},{13,9},{1... | collective-permute-start | bytes 786440 | tf_op jit(solution)/shard_map/ppermute | solution.py:17
  450.0 10.2 %collective-permute-start.33 = (bf16[1,1,2,64,1024]{4,3,2,1,0:T(8,128)(2,1)S(1)}, bf16[1,1,2,64,1024]{4,3,2,1,0:T(8,128)(2,1)S(1)}, u32[]{:S(2)}, u32[]{:S(2)}) collective-permute-start(bf16[1,1,2,64,1024]{4,3,2,1,0:T(8,128)(2,1)S(1)} %broadcast_select_fusion.7), channel_id=1, source_target_pairs={{8,0},{9,1},{10,2},{11,3},{12,4},{13,5},{14,6},{15,7},{0,8},{1,9},... | collective-permute-start | bytes 786440 | tf_op jit(solution)/shard_map/ppermute | solution.py:17
  455.0 9.2 %collective-permute-start.17 = (bf16[1,1,2,64,1024]{4,3,2,1,0:T(8,128)(2,1)S(1)}, bf16[1,1,2,64,1024]{4,3,2,1,0:T(8,128)(2,1)S(1)}, u32[]{:S(2)}, u32[]{:S(2)}) collective-permute-start(bf16[1,1,2,64,1024]{4,3,2,1,0:T(8,128)(2,1)S(1)} %broadcast_select_fusion.15), channel_id=1, source_target_pairs={{8,0},{9,1},{10,2},{11,3},{12,4},{13,5},{14,6},{15,7},{0,8},{1,9},... | collective-permute-start | bytes 786440 | tf_op jit(solution)/shard_map/ppermute | solution.py:17
  (8 other events, 111.9 us)
Sparse Core Ops, SparseCore 0:
  15.0 189.0 all-gather.8
  207.2 235.8 all-gather.4
  445.3 50.0 all-gather.10
  497.4 41.8 all-gather.6
